TPU v7x, 32 devices: a whole 2x2x4 slice. The times are simulated.
32 devices in a mesh: gx: 4 (over y, x), gy: 8 (over z, core).
Axes of the slice: x: 2, y: 2, z: 4, core: 2. Of those that a mesh axis runs over, the one named last changes fastest.
Arguments:
- fields: bfloat16 [8, 64, 128, 192], P(None, 'gx', 'gy'), may hold values from -6 to 6
- gain_window: float32 [192], replicated, may hold values from 0.1 to 1.9
- mixer_fine: bfloat16 [192, 576], replicated, may hold values from -3 to 3
- output_fine: bfloat16 [192, 192], replicated, may hold values from -0.4375 to 0.4375
- gain_hidden: float32 [192], replicated, may hold values from 0.1 to 1.9
- expand: bfloat16 [192, 768], replicated, may hold values from -0.4375 to 0.4375
- contract: bfloat16 [768, 192], replicated, may hold values from -0.21875 to 0.21875
- gain_merge: float32 [768], replicated, may hold values from 0.1 to 1.9
- merge_weight: bfloat16 [768, 384], replicated, may hold values from -0.21875 to 0.21875
- gain_coarse: float32 [384], replicated, may hold values from 0.1 to 1.9
- mixer_coarse: bfloat16 [384, 1152], replicated, may hold values from -2.1 to 2.1
- output_coarse: bfloat16 [384, 384], replicated, may hold values from -0.3125 to 0.3125
Outputs:
- merged: bfloat16 [8, 32, 64, 384], P(None, 'gx', 'gy')
- coarse: bfloat16 [8, 32, 64, 384], P(None, 'gx', 'gy')
All inputs are finite; a program needn't handle non-finite values.
Results may differ from a plain program's by a relative error of at most 0.019.
Values may be sent and summed in bfloat16 or wider, within the bound.
A program may use at most 128 MiB of HBM per device.

v0:
```python
import math

import jax
import jax.numpy as jnp
from jax import lax
from jax.sharding import PartitionSpec as P

HEAD = 32


epsilon = 1e-05


def from_behind(shard, axis, by):
    count = lax.axis_size(axis)
    return lax.ppermute(shard, axis, [(i, (i + by) % count) for i in range(count)])


def swapped(value, axis, stride):
    mask = 2**stride
    pairs = [(source, source ^ mask) for source in range(lax.axis_size(axis))]
    return lax.ppermute(value, axis, pairs)


def normalize(values, scaling):
    values = values.astype(jnp.float32)
    center = values - jnp.mean(values, -1, keepdims=True)
    spread = jnp.mean(center * center, -1, keepdims=True)
    return center * lax.rsqrt(spread + epsilon) * scaling


def attend(query_rows, key_rows, value_rows, head_count):
    windows, length, channels = query_rows.shape
    head_size = channels // head_count
    split_query = query_rows.reshape(windows, length, head_count, head_size)
    split_keys = key_rows.reshape(windows, -1, head_count, head_size)
    split_values = value_rows.reshape(windows, -1, head_count, head_size)
    scores = jnp.einsum(
        "nqhd,nkhd->nhqk", split_query, split_keys, preferred_element_type=jnp.float32
    ) / math.sqrt(head_size)
    highest = jnp.max(scores, -1, keepdims=True)
    powers = jnp.exp(scores - highest)
    attention = (powers / jnp.sum(powers, -1, keepdims=True)).astype(jnp.bfloat16)
    context = jnp.einsum(
        "nhqk,nkhd->nqhd", attention, split_values, preferred_element_type=jnp.float32
    )
    return context.reshape(windows, length, channels).astype(jnp.bfloat16)


def attention_layer(tokens, scaling, mixer, output_weight, head_count):
    channels = tokens.shape[-1]
    normed = normalize(tokens, scaling).astype(jnp.bfloat16)
    projected = jnp.dot(normed, mixer, preferred_element_type=jnp.float32).astype(jnp.bfloat16)
    context = attend(
        projected[..., :channels],
        projected[..., channels : 2 * channels],
        projected[..., 2 * channels :],
        head_count,
    )
    update = jnp.dot(context, output_weight, preferred_element_type=jnp.float32)
    return (tokens.astype(jnp.float32) + update).astype(jnp.bfloat16)


def feed_forward(tokens, scaling, expand, contract):
    normed = normalize(tokens, scaling).astype(jnp.bfloat16)
    hidden = jax.nn.gelu(
        jnp.dot(normed, expand, preferred_element_type=jnp.float32), approximate=False
    ).astype(jnp.bfloat16)
    return (
        tokens.astype(jnp.float32) + jnp.dot(hidden, contract, preferred_element_type=jnp.float32)
    ).astype(jnp.bfloat16)


def merge_patches(tokens, scaling, merge_weight):
    samples, height, breadth, channels = tokens.shape
    patches = tokens.reshape(samples, height // 2, 2, breadth // 2, 2, channels).transpose(
        0, 1, 3, 4, 2, 5
    )
    patches = patches.reshape(samples, height // 2, breadth // 2, 4 * channels)
    normed = normalize(patches, scaling).astype(jnp.bfloat16)
    return jnp.dot(normed, merge_weight, preferred_element_type=jnp.float32).astype(jnp.bfloat16)


def roll_ahead(tokens):
    offset = tokens.shape[1] // 2
    following = from_behind(tokens[:, :offset], "gx", -1)
    shifted = jnp.concatenate([tokens[:, offset:], following], axis=1)
    beside = from_behind(shifted[:, :, :offset], "gy", -1)
    return jnp.concatenate([shifted[:, :, offset:], beside], axis=2)


def roll_return(tokens):
    offset = tokens.shape[1] // 2
    preceding = from_behind(tokens[:, :, offset:], "gy", 1)
    shifted = jnp.concatenate([preceding, tokens[:, :, :offset]], axis=2)
    previous = from_behind(shifted[:, offset:], "gx", 1)
    return jnp.concatenate([previous, shifted[:, :offset]], axis=1)


def shards(
    fields,
    gain_window,
    mixer_fine,
    output_fine,
    gain_hidden,
    expand,
    contract,
    gain_merge,
    merge_weight,
    gain_coarse,
    mixer_coarse,
    output_coarse,
):
    samples = fields.shape[0]
    length = fields.shape[1]
    channels = fields.shape[-1]
    head_fine = channels // HEAD
    shifted = roll_ahead(fields)
    attended = attention_layer(
        shifted.reshape(samples, length * length, channels),
        gain_window,
        mixer_fine,
        output_fine,
        head_fine,
    )
    restored = roll_return(attended.reshape(samples, length, length, channels))
    refined = feed_forward(restored, gain_hidden, expand, contract)
    merged = merge_patches(refined, gain_merge, merge_weight)
    coarse_side = merged.shape[1]
    coarse_width = merged.shape[-1]
    head_coarse = coarse_width // HEAD
    flattened = merged.reshape(samples, coarse_side * coarse_side, coarse_width)
    normed_coarse = normalize(flattened, gain_coarse).astype(jnp.bfloat16)
    queries_coarse = jnp.dot(
        normed_coarse, mixer_coarse[:, :coarse_width], preferred_element_type=jnp.float32
    ).astype(jnp.bfloat16)
    column_pair = jnp.concatenate([normed_coarse, swapped(normed_coarse, "gx", 0)], axis=1)
    grouped = jnp.concatenate([column_pair, swapped(column_pair, "gy", 0)], axis=1)
    gathered = jnp.dot(
        grouped, mixer_coarse[:, coarse_width:], preferred_element_type=jnp.float32
    ).astype(jnp.bfloat16)
    context_coarse = attend(
        queries_coarse, gathered[..., :coarse_width], gathered[..., coarse_width:], head_coarse
    )
    update_coarse = jnp.dot(context_coarse, output_coarse, preferred_element_type=jnp.float32)
    coarse = (
        (flattened.astype(jnp.float32) + update_coarse).astype(jnp.bfloat16).reshape(merged.shape)
    )
    return (merged, coarse)


def solution(mesh):
    in_specs = (P(None, "gx", "gy", None), P(), P(), P(), P(), P(), P(), P(), P(), P(), P(), P())
    out_specs = (P(None, "gx", "gy", None), P(None, "gx", "gy", None))
    return jax.shard_map(shards, mesh=mesh, in_specs=in_specs, out_specs=out_specs, check_vma=False)
```

profile of v0, /device:TPU:0, one launch (start us, length us, event | category | flops | bytes accessed | tf_op | source)
XLA Modules:
  0.0 133.6 jit_solution(6458753648603266375)
XLA Ops:
  0.6 0.0 copy-start
  0.6 1.4 %fusion.121 = (bf16[8,8,16,192]{3,2,1,0:T(8,128)(2,1)S(1)}, bf16[8,8,16,192]{3,2,1,0:T(8,128)(2,1)S(1)}) fusion(bf16[8,16,16,192]{3,2,1,0:T(8,128)(2,1)} %param.12), kind=kLoop, calls=%fused_computation.160 | loop fusion | bytes 1572864 | tf_op jit(solution)/shard_map/slice | solution.py:87
  2.0 0.0 copy-start.7
  2.0 0.0 copy-start.10
  2.0 4.0 %collective-permute-start = (bf16[8,8,16,192]{3,2,1,0:T(8,128)(2,1)S(1)}, bf16[8,8,16,192]{3,2,1,0:T(8,128)(2,1)S(1)}, u32[]{:S(2)}, u32[]{:S(2)}) collective-permute-start(bf16[8,8,16,192]{3,2,1,0:T(8,128)(2,1)S(1)} %get-tuple-element.14), channel_id=1, source_target_pairs={{0,24},{8,0},{16,8},{24,16},{1,25},{9,1},{17,9},{25,17},{2,26},{10... | collective-permute-start | bytes 1179656 | tf_op jit(solution)/shard_map/ppermute | solution.py:16
  6.0 11.2 %collective-permute-done = bf16[8,8,16,192]{3,2,1,0:T(8,128)(2,1)S(1)} collective-permute-done((bf16[8,8,16,192]{3,2,1,0:T(8,128)(2,1)S(1)}, bf16[8,8,16,192]{3,2,1,0:T(8,128)(2,1)S(1)}, u32[]{:S(2)}, u32[]{:S(2)}) %collective-permute-start) | collective-permute-done | bytes 393248 | tf_op jit(solution)/shard_map/ppermute | solution.py:16
  17.2 0.2 fusion.71
  17.4 2.3 %collective-permute-start.1 = (bf16[8,16,8,192]{3,2,1,0:T(8,128)(2,1)S(1)}, bf16[8,16,8,192]{3,2,1,0:T(8,128)(2,1)S(1)}, u32[]{:S(2)}, u32[]{:S(2)}) collective-permute-start(bf16[8,16,8,192]{3,2,1,0:T(8,128)(2,1)S(1)} %get-tuple-element.12), channel_id=1, source_target_pairs={{0,7},{1,0},{2,1},{3,2},{4,3},{5,4},{6,5},{7,6},{8,15},{9,8},{10,9... | collective-permute-start | bytes 1179656 | tf_op jit(solution)/shard_map/ppermute | solution.py:16
  19.7 6.7 %collective-permute-done.1 = bf16[8,16,8,192]{3,2,1,0:T(8,128)(2,1)S(1)} collective-permute-done((bf16[8,16,8,192]{3,2,1,0:T(8,128)(2,1)S(1)}, bf16[8,16,8,192]{3,2,1,0:T(8,128)(2,1)S(1)}, u32[]{:S(2)}, u32[]{:S(2)}) %collective-permute-start.1) | collective-permute-done | bytes 393248 | tf_op jit(solution)/shard_map/ppermute | solution.py:16
  26.4 0.3 fusion.74
  26.7 0.1 div.57
  26.8 0.7 multiply_reduce_fusion.3
  27.5 0.1 rsqrt.39
  27.6 1.3 maximum_convert_fusion
  28.9 1.7 %copy.27 = f32[8,256,192]{1,2,0:T(8,128)} copy(f32[8,256,192]{2,1,0:T(8,128)S(1)} %bitcast.81) | data formatting | bytes 3145728 | tf_op jit(solution)/shard_map/convert_element_type | solution.py:61
  30.6 1.6 %convolution_convert_fusion.1 = bf16[8,256,576]{1,2,0:T(8,128)(2,1)S(1)} fusion(f32[8,256,192]{2,1,0:T(8,128)S(1)} %bitcast.82, f32[192]{0:T(256)S(1)} %copy-done.10, f32[8,256]{1,0:T(8,128)S(1)} %rsqrt.39, f32[8,256]{1,0:T(8,128)S(1)} %div.57, bf16[192,576]{1,0:T(8,128)(2,1)S(1)} %copy-done.7), kind=kOutput, calls=%fused_computation.52 | convolution fusion | flops 455737344 | bytes 4170496 | tf_op jit(solution)/shard_map/dot_general | solution.py:53
  32.2 0.2 fusion.119
  32.4 7.1 %fusion.122 = (f32[8,6,256]{2,1,0:T(8,128)S(1)}, f32[8,6,256,256]{2,3,1,0:T(8,128)}) fusion(bf16[8,256,6,32]{1,3,2,0:T(8,128)(2,1)S(1)} %bitcast.89, bf16[8,256,6,32]{1,3,2,0:T(8,128)(2,1)S(1)} %bitcast.88), kind=kOutput, calls=%fused_computation.161 | convolution fusion | flops 210764032 | bytes 14204928 | tf_op jit(solution)/shard_map/sub | solution.py:42
  39.5 5.9 %fusion.41 = bf16[8,6,32,256]{3,2,1,0:T(8,128)(2,1)S(1)} fusion(bf16[8,256,6,32]{1,3,2,0:T(8,128)(2,1)S(1)} %bitcast.87, f32[8,6,256,256]{2,3,1,0:T(8,128)} %get-tuple-element.16, f32[8,6,256]{2,1,0:T(8,128)S(1)} %get-tuple-element.15), kind=kOutput, calls=%fused_computation.64 | convolution fusion | flops 208011264 | bytes 14204928 | tf_op jit(solution)/shard_map/nhqk,nkhd->nqhd/dot_general | solution.py:44
  45.4 0.0 copy-done.8
  45.4 0.4 fusion.81
  45.9 0.0 copy-start.11
  45.9 0.0 copy-start.14
  45.9 0.3 add_convert_fusion
  46.2 0.5 copy.28
  46.7 0.1 fusion.120
  46.8 0.1 collective-permute-start.2
  46.9 10.5 %collective-permute-done.2 = bf16[8,16,8,192]{3,2,1,0:T(8,128)(2,1)S(1)} collective-permute-done((bf16[8,16,8,192]{3,2,1,0:T(8,128)(2,1)S(1)}, bf16[8,16,8,192]{3,2,1,0:T(8,128)(2,1)S(1)}, u32[]{:S(2)}, u32[]{:S(2)}) %collective-permute-start.2) | collective-permute-done | bytes 393248 | tf_op jit(solution)/shard_map/ppermute | solution.py:16
  57.4 0.1 fusion.70
  57.5 2.4 %collective-permute-start.3 = (bf16[8,8,16,192]{3,2,1,0:T(8,128)(2,1)S(1)}, bf16[8,8,16,192]{3,2,1,0:T(8,128)(2,1)S(1)}, u32[]{:S(2)}, u32[]{:S(2)}) collective-permute-start(bf16[8,8,16,192]{3,2,1,0:T(8,128)(2,1)S(1)} %fusion.70), channel_id=1, source_target_pairs={{0,8},{8,16},{16,24},{24,0},{1,9},{9,17},{17,25},{25,1},{2,10},{10... | collective-permute-start | bytes 1179656 | tf_op jit(solution)/shard_map/ppermute | solution.py:16
  60.0 8.3 %collective-permute-done.3 = bf16[8,8,16,192]{3,2,1,0:T(8,128)(2,1)S(1)} collective-permute-done((bf16[8,8,16,192]{3,2,1,0:T(8,128)(2,1)S(1)}, bf16[8,8,16,192]{3,2,1,0:T(8,128)(2,1)S(1)}, u32[]{:S(2)}, u32[]{:S(2)}) %collective-permute-start.3) | collective-permute-done | bytes 393248 | tf_op jit(solution)/shard_map/ppermute | solution.py:16
  68.3 0.3 convert_reduce_fusion
  68.6 0.7 fusion.27
  69.3 0.0 copy-start.12
  69.4 2.5 %fusion.21 = (u16[8,16,768]{2,1,0:T(8,128)(2,1)S(1)}, u16[8,16,768]{2,1,0:T(8,128)(2,1)S(1)}, f32[8,16,16,768]{3,2,1,0:T(8,128)S(1)}) fusion(bf16[192,768]{1,0:T(8,128)(2,1)S(1)} %copy-done.11, f32[192]{0:T(256)S(1)} %copy-done.14, f32[8,16,16]{2,1,0:T(8,128)S(1)} %add_rsqrt_fusion, f32[8,16,16]{2,1,0:T(8,128)S(1)} %broadcast_multiply_fusion, ...), kind=kOutput, calls=%fused_computation.39 | convolution fusion | flops 628162560 | bytes 8176384 | tf_op jit(solution)/shard_map/dot_general | solution.py:67
  71.9 16.0 %fusion.44 = f32[8,16,16,192]{3,2,1,0:T(8,128)} fusion(f32[8,16,16,768]{3,2,1,0:T(8,128)S(1)} %get-tuple-element.17, u16[8,16,768]{2,1,0:T(8,128)(2,1)S(1)} %get-tuple-element.3, u16[8,16,768]{2,1,0:T(8,128)(2,1)S(1)} %get-tuple-element.2, bf16[768,192]{0,1:T(8,128)(2,1)S(1)} %copy-done.12, bf16[8,16,8,192]{3,2,1,0:T(8,128)(2,1)S(1)} %get-tuple-element.10, ...), kind=kOutput, calls=%fused_computation.65 | convolution fusion | flops 717619200 | bytes 9732096 | tf_op jit(solution)/shard_map/dot_general | solution.py:70
  87.9 2.5 %reshape.148 = f32[8,8,2,8,2,192]{5,4,3,2,1,0:T(2,128)S(1)} reshape(f32[8,16,16,192]{3,2,1,0:T(8,128)} %fusion.44) | data formatting | bytes 3145728 | tf_op jit(solution)/shard_map/convert_element_type | solution.py:26
  90.4 0.0 copy-start.13
  90.4 1.2 bitcast_reduce_fusion
  91.7 0.0 copy-start.9
  91.7 2.3 %multiply_reduce_fusion.2 = f32[8,8,8]{2,1,0:T(8,128)S(1)} fusion(f32[8,8,8]{2,1,0:T(8,128)S(1)} %broadcast_multiply_fusion.3, f32[8,8,2,8,2,192]{5,4,3,2,1,0:T(2,128)S(1)} %reshape.148), kind=kLoop, calls=%fused_computation.49 | loop fusion | flops 1179136 | bytes 1576960 | tf_op jit(solution)/shard_map/reduce_sum | solution.py:28
  94.0 3.2 %copy.29 = f32[8,8,8,2,2,192]{5,4,3,2,1,0:T(2,128)} copy(f32[8,8,8,2,2,192]{5,3,2,4,1,0:T(2,128)S(1)} %bitcast.80) | data formatting | bytes 3145728 | tf_op jit(solution)/shard_map/convert_element_type | solution.py:26
  97.2 3.4 %reshape.145 = f32[8,8,8,768]{3,2,1,0:T(8,128)S(1)} reshape(f32[8,8,8,2,2,192]{5,4,3,2,1,0:T(2,128)} %copy.29) | data formatting | bytes 3145728 | tf_op jit(solution)/shard_map/convert_element_type | solution.py:26
  100.7 0.7 convert_reduce_fusion.1
  101.4 0.0 copy-start.3
  101.4 0.1 div.68
  101.5 0.3 fusion.63
  101.8 0.1 rsqrt.43
  101.9 0.2 fusion.61
  102.1 0.9 collective-permute-start.4
  103.0 6.9 %collective-permute-done.4 = bf16[8,64,384]{2,1,0:T(8,128)(2,1)S(1)} collective-permute-done((bf16[8,64,384]{2,1,0:T(8,128)(2,1)S(1)}, bf16[8,64,384]{2,1,0:T(8,128)(2,1)S(1)}, u32[]{:S(2)}, u32[]{:S(2)}) %collective-permute-start.4) | collective-permute-done | bytes 393248 | tf_op jit(solution)/shard_map/ppermute | solution.py:22
  109.9 0.1 pad_maximum_fusion.1
  110.0 0.7 copy-done.5
  110.7 0.0 collective-permute-start.5
  110.7 1.3 %convolution_convert_fusion.3 = bf16[8,64,384]{2,1,0:T(8,128)(2,1)S(1)} fusion(bf16[8,64,384]{2,1,0:T(8,128)(2,1)S(1)} %fusion.61, bf16[384,1152]{1,0:T(8,128)(2,1)} %param.22), kind=kOutput, calls=%fused_computation.69 | convolution fusion | flops 151191552 | bytes 1081344 | tf_op jit(solution)/shard_map/dot_general | solution.py:134
  112.0 0.4 copy.31
  112.4 0.7 collective-permute-done.5
  113.1 3.2 %convolution_convert_fusion = bf16[8,256,768]{2,1,0:T(8,128)(2,1)S(1)} fusion(bf16[8,128,384]{2,1,0:T(8,128)(2,1)} %collective-permute-done.5, bf16[8,64,384]{2,1,0:T(8,128)(2,1)} %copy-done.5, bf16[8,64,384]{2,1,0:T(8,128)(2,1)S(1)} %fusion.61, bf16[384,1152]{1,0:T(8,128)(2,1)} %param.22), kind=kOutput, calls=%fused_computation.44 | convolution fusion | flops 1214251008 | bytes 5308416 | tf_op jit(solution)/shard_map/dot_general | solution.py:139
  116.3 1.7 %fusion.118 = (bf16[8,256,384]{2,1,0:T(8,128)(2,1)}, bf16[8,256,384]{2,1,0:T(8,128)(2,1)S(1)}) fusion(bf16[8,256,768]{2,1,0:T(8,128)(2,1)S(1)} %convolution_convert_fusion), kind=kLoop, calls=%fused_computation.157 | loop fusion | bytes 6291456 | tf_op jit(solution)/shard_map/slice | solution.py:143
  118.0 2.6 %copy.32 = bf16[8,256,384]{1,2,0:T(8,128)(2,1)} copy(bf16[8,256,384]{2,1,0:T(8,128)(2,1)} %get-tuple-element.4) | data formatting | bytes 3145728 | tf_op jit(solution)/shard_map/slice | solution.py:143
  120.5 1.7 %copy.30 = bf16[8,256,384]{1,2,0:T(8,128)(2,1)} copy(bf16[8,256,384]{2,1,0:T(8,128)(2,1)S(1)} %get-tuple-element.5) | data formatting | bytes 3145728 | tf_op jit(solution)/shard_map/slice | solution.py:143
  122.2 6.2 %fusion.123 = (f32[8,12,64]{2,1,0:T(8,128)S(1)}, f32[8,12,64,256]{3,2,1,0:T(8,128)}) fusion(bf16[8,64,12,32]{1,3,2,0:T(8,128)(2,1)S(1)} %bitcast.85, bf16[8,256,12,32]{1,3,2,0:T(8,128)(2,1)} %bitcast.83), kind=kOutput, calls=%fused_computation.162 | convolution fusion | flops 105382144 | bytes 8282112 | tf_op jit(solution)/shard_map/sub | solution.py:42
  128.4 3.9 %fusion.40 = bf16[8,12,32,64]{3,2,1,0:T(8,128)(2,1)S(1)} fusion(bf16[8,256,12,32]{1,3,2,0:T(8,128)(2,1)S(1)} %bitcast.86, f32[8,12,64,256]{3,2,1,0:T(8,128)} %get-tuple-element.21, f32[8,12,64]{2,1,0:T(8,128)S(1)} %get-tuple-element.20), kind=kOutput, calls=%fused_computation.63 | convolution fusion | flops 104005632 | bytes 8282112 | tf_op jit(solution)/shard_map/nhqk,nkhd->nqhd/dot_general | solution.py:44
  132.3 1.2 fusion.48
  (27 shorter events, 0.1 us)
Async XLA Ops:
  0.6 100.0 %copy-start = (bf16[768,384]{1,0:T(8,128)(2,1)S(1)}, bf16[768,384]{1,0:T(8,128)(2,1)}, u32[]{:S(2)}) copy-start(bf16[768,384]{1,0:T(8,128)(2,1)} %param.20) | copy-start | bytes 1769476
  2.0 28.6 %copy-start.7 = (bf16[192,576]{1,0:T(8,128)(2,1)S(1)}, bf16[192,576]{1,0:T(8,128)(2,1)}, u32[]{:S(2)}) copy-start(bf16[192,576]{1,0:T(8,128)(2,1)} %param.14) | copy-start | bytes 663556
  2.0 28.6 %copy-start.10 = (f32[192]{0:T(256)S(1)}, f32[192]{0:T(256)}, u32[]{:S(2)}) copy-start(f32[192]{0:T(256)} %param.13) | copy-start | bytes 2308
  2.0 15.2 %collective-permute-start = (bf16[8,8,16,192]{3,2,1,0:T(8,128)(2,1)S(1)}, bf16[8,8,16,192]{3,2,1,0:T(8,128)(2,1)S(1)}, u32[]{:S(2)}, u32[]{:S(2)}) collective-permute-start(bf16[8,8,16,192]{3,2,1,0:T(8,128)(2,1)S(1)} %get-tuple-element.14), channel_id=1, source_target_pairs={{0,24},{8,0},{16,8},{24,16},{1,25},{9,1},{17,9},{25,17},{2,26},{10... | collective-permute-start | bytes 1179656 | tf_op jit(solution)/shard_map/ppermute | solution.py:16
  17.4 9.0 %collective-permute-start.1 = (bf16[8,16,8,192]{3,2,1,0:T(8,128)(2,1)S(1)}, bf16[8,16,8,192]{3,2,1,0:T(8,128)(2,1)S(1)}, u32[]{:S(2)}, u32[]{:S(2)}) collective-permute-start(bf16[8,16,8,192]{3,2,1,0:T(8,128)(2,1)S(1)} %get-tuple-element.12), channel_id=1, source_target_pairs={{0,7},{1,0},{2,1},{3,2},{4,3},{5,4},{6,5},{7,6},{8,15},{9,8},{10,9... | collective-permute-start | bytes 1179656 | tf_op jit(solution)/shard_map/ppermute | solution.py:16
  26.4 1.2 copy-start.2
  39.5 5.9 %copy-start.8 = (bf16[192,192]{1,0:T(8,128)(2,1)S(1)}, bf16[192,192]{1,0:T(8,128)(2,1)}, u32[]{:S(2)}) copy-start(bf16[192,192]{1,0:T(8,128)(2,1)} %param.15) | copy-start | bytes 221188
  39.5 6.3 %copy-start.1 = (f32[8,256,192]{1,2,0:T(8,128)S(1)}, f32[8,256,192]{1,2,0:T(8,128)}, u32[]{:S(2)}) copy-start(f32[8,256,192]{1,2,0:T(8,128)} %copy.27) | copy-start | bytes 4718596
  45.9 23.5 %copy-start.11 = (bf16[192,768]{1,0:T(8,128)(2,1)S(1)}, bf16[192,768]{1,0:T(8,128)(2,1)}, u32[]{:S(2)}) copy-start(bf16[192,768]{1,0:T(8,128)(2,1)} %param.17) | copy-start | bytes 884740
  45.9 23.5 %copy-start.14 = (f32[192]{0:T(256)S(1)}, f32[192]{0:T(256)}, u32[]{:S(2)}) copy-start(f32[192]{0:T(256)} %param.16) | copy-start | bytes 2308
  46.8 10.6 %collective-permute-start.2 = (bf16[8,16,8,192]{3,2,1,0:T(8,128)(2,1)S(1)}, bf16[8,16,8,192]{3,2,1,0:T(8,128)(2,1)S(1)}, u32[]{:S(2)}, u32[]{:S(2)}) collective-permute-start(bf16[8,16,8,192]{3,2,1,0:T(8,128)(2,1)S(1)} %get-tuple-element.9), channel_id=1, source_target_pairs={{0,1},{1,2},{2,3},{3,4},{4,5},{5,6},{6,7},{7,0},{8,9},{9,10},{10,1... | collective-permute-start | bytes 1179656 | tf_op jit(solution)/shard_map/ppermute | solution.py:16
  57.5 10.7 %collective-permute-start.3 = (bf16[8,8,16,192]{3,2,1,0:T(8,128)(2,1)S(1)}, bf16[8,8,16,192]{3,2,1,0:T(8,128)(2,1)S(1)}, u32[]{:S(2)}, u32[]{:S(2)}) collective-permute-start(bf16[8,8,16,192]{3,2,1,0:T(8,128)(2,1)S(1)} %fusion.70), channel_id=1, source_target_pairs={{0,8},{8,16},{16,24},{24,0},{1,9},{9,17},{17,25},{25,1},{2,10},{10... | collective-permute-start | bytes 1179656 | tf_op jit(solution)/shard_map/ppermute | solution.py:16
  69.3 2.5 %copy-start.12 = (bf16[768,192]{0,1:T(8,128)(2,1)S(1)}, bf16[768,192]{0,1:T(8,128)(2,1)}, u32[]{:S(2)}) copy-start(bf16[768,192]{0,1:T(8,128)(2,1)} %param.18) | copy-start | bytes 884740
  90.4 10.2 %copy-start.13 = (f32[768]{0:T(1024)S(1)}, f32[768]{0:T(1024)}, u32[]{:S(2)}) copy-start(f32[768]{0:T(1024)} %param.19) | copy-start | bytes 9220
  91.7 10.2 %copy-start.9 = (f32[384]{0:T(512)S(1)}, f32[384]{0:T(512)}, u32[]{:S(2)}) copy-start(f32[384]{0:T(512)} %param.21) | copy-start | bytes 4612
  101.4 30.9 %copy-start.3 = (bf16[8,8,8,384]{3,2,1,0:T(8,128)(2,1)}, bf16[8,8,8,384]{3,2,1,0:T(8,128)(2,1)S(1)}, u32[]{:S(2)}) copy-start(bf16[8,8,8,384]{3,2,1,0:T(8,128)(2,1)S(1)} %get-tuple-element.19) | copy-start | bytes 1179652
  102.1 7.8 %collective-permute-start.4 = (bf16[8,64,384]{2,1,0:T(8,128)(2,1)S(1)}, bf16[8,64,384]{2,1,0:T(8,128)(2,1)S(1)}, u32[]{:S(2)}, u32[]{:S(2)}) collective-permute-start(bf16[8,64,384]{2,1,0:T(8,128)(2,1)S(1)} %fusion.61), channel_id=1, source_target_pairs={{0,8},{8,0},{16,24},{24,16},{1,9},{9,1},{17,25},{25,17},{2,10},{10... | collective-permute-start | bytes 1179656 | tf_op jit(solution)/shard_map/ppermute | solution.py:22
  109.9 0.7 copy-start.5
  110.7 2.4 %collective-permute-start.5 = (bf16[8,128,384]{2,1,0:T(8,128)(2,1)S(1)}, bf16[8,128,384]{2,1,0:T(8,128)(2,1)}, u32[]{:S(2)}, u32[]{:S(2)}) collective-permute-start(bf16[8,128,384]{2,1,0:T(8,128)(2,1)S(1)} %pad_maximum_fusion.1), channel_id=1, source_target_pairs={{0,1},{1,0},{2,3},{3,2},{4,5},{5,4},{6,7},{7,6},{8,9},{9,8},{10,11... | collective-permute-start | bytes 2359304 | tf_op jit(solution)/shard_map/ppermute | solution.py:22
  122.2 6.2 %copy-start.4 = (bf16[8,256,384]{1,2,0:T(8,128)(2,1)S(1)}, bf16[8,256,384]{1,2,0:T(8,128)(2,1)}, u32[]{:S(2)}) copy-start(bf16[8,256,384]{1,2,0:T(8,128)(2,1)} %copy.30) | copy-start | bytes 4718596
  128.4 3.9 %copy-start.6 = (bf16[384,384]{1,0:T(8,128)(2,1)S(1)}, bf16[384,384]{1,0:T(8,128)(2,1)}, u32[]{:S(2)}) copy-start(bf16[384,384]{1,0:T(8,128)(2,1)} %param.23) | copy-start | bytes 884740
where the time goes:
time: 136 us; the launch traced here: 134 us
  matrix products  50.1 us (37%)
  waiting for transfers between devices  44.3 us (33%)
  local copies, waits for them, and re-layouts  20.4 us (15%)
  starting transfers between devices  9.69 us (7%)
  other arithmetic  8.07 us (6%)
    ppermute x4, waiting for transfers between devices, from_behind(): lax.ppermute(shard, axis, [(i, (i + by) % count) for i in range(count)])  36.7 us
    dot_general x1, matrix products, feed_forward(): jnp.dot(hidden, contract, preferred_element_type=jnp.float32)  16 us
    sub x2, matrix products, attend(): powers = jnp.exp(scores - highest)  13.3 us
    dot_general x2, matrix products, attend(): jnp.einsum('nhqk,nkhd->nqhd', attention, split_values, preferred_element_...  9.76 us
    convert_element_type x3, local copies, waits for them, and re-layouts, normalize(): values = values.astype(jnp.float32)  9.16 us
    ppermute x4, starting transfers between devices, from_behind(): lax.ppermute(shard, axis, [(i, (i + by) % count) for i in range(count)])  8.75 us
    ppermute x2, waiting for transfers between devices, swapped(): return lax.ppermute(value, axis, pairs)  7.57 us
    slice x2, local copies, waits for them, and re-layouts, shards(): gathered[..., :coarse_width]  4.22 us
  transfers between devices with their start and end apart: 6, of which 6 were waited for; matrix products, arithmetic and copies ran while one was open for 1% of the time, Pallas kernels for 0%

commit v1 on v0

v1 whole, which is shorter than its diff:
```python
import functools
import math

import jax
import jax.numpy as jnp
from jax import lax
from jax.experimental import pallas as pl
from jax.experimental.pallas import tpu as pltpu
from jax.sharding import PartitionSpec as P

HEAD = 32
LANES = 128
EPSILON = 1e-05
F32 = jnp.float32
BF16 = jnp.bfloat16
MESH = pl.DeviceIdType.MESH


def dot(a, b):
    return jnp.dot(a, b, preferred_element_type=F32)


def normalize(values, gain):
    center = values - jnp.mean(values, -1, keepdims=True)
    spread = jnp.mean(center * center, -1, keepdims=True)
    return (center * lax.rsqrt(spread + EPSILON) * gain).astype(BF16)


def gelu(x):
    return 0.5 * x * (1.0 + lax.erf(x * (1.0 / math.sqrt(2.0))))


def attention(queries, keys, values):
    channels = queries.shape[-1]
    factor = math.log2(math.e) / math.sqrt(HEAD)
    groups = []
    for low in range(0, channels, LANES):
        width = min(LANES, channels - low)
        q, k, v = (t[:, low : low + width] for t in (queries, keys, values))
        owner = lax.broadcasted_iota(jnp.int32, (1, width), 1) // HEAD
        context = None
        for head in range(width // HEAD):
            mine = owner == head
            scores = lax.dot_general(
                q * mine.astype(F32).astype(BF16), k, (((1,), (1,)), ((), ())),
                preferred_element_type=F32,
            )
            highest = jnp.max(scores, -1, keepdims=True)
            powers = jnp.exp2((scores - highest) * factor)
            total = jnp.sum(powers, -1, keepdims=True)
            part = dot(powers.astype(BF16), v) * (1.0 / total)
            context = part if context is None else jnp.where(mine, part, context)
        groups.append(context.astype(BF16))
    return groups


def project(groups, weight_ref):
    total = None
    for index, group in enumerate(groups):
        part = dot(group, weight_ref[index * LANES : index * LANES + group.shape[-1], :])
        total = part if total is None else total + part
    return total


def kernel(
    nx, ny,
    fields, gain_window, mixer_fine, output_fine, gain_hidden, expand, contract,
    gain_merge, merge_weight, gain_coarse, mixer_coarse, output_coarse,
    merged_out, coarse_out,
    fbuf, mbuf, mhome, cbuf, obuf, wsplit, perm_fine, perm_coarse,
    f_send, f_recv, m_send, m_recv, c_send, c_recv, o_send, o_recv,
):
    samples, _, half, _, channels = fbuf.shape
    side = 2 * half
    tokens = side * side
    quarter = half // 2
    piece = quarter * quarter
    patch = 4 * piece
    wide = merged_out.shape[-1]
    x = lax.axis_index("gx")
    y = lax.axis_index("gy")

    def at(dx, dy):
        return (lax.rem(x + dx + nx, nx), lax.rem(y + dy + ny, ny))

    def field_copy(n, a, b):
        slot = (1 - a) * 2 + (1 - b)
        source = fields.at[n, pl.ds(a * half, half), b]
        target = fbuf.at[n, slot]
        if a == 1 and b == 1:
            return pltpu.make_async_copy(source, target, f_recv.at[n])
        return pltpu.make_async_remote_copy(
            source, target, f_send.at[n, slot], f_recv.at[n],
            device_id=at(a - 1, b - 1), device_id_type=MESH,
        )

    ORDER = ((0, 0), (0, 1), (1, 0), (1, 1))

    barrier = pltpu.get_barrier_semaphore()
    reach = [(dx, dy) for dx in range(-2, 3) for dy in range(-2, 3) if (dx, dy) != (0, 0)]
    for dx, dy in reach:
        pl.semaphore_signal(barrier, inc=1, device_id=at(dx, dy), device_id_type=MESH)
    pl.semaphore_wait(barrier, len(reach))

    def start_fields(n, carry):
        for a, b in ORDER:
            field_copy(n, a, b).start()
        return carry

    lax.fori_loop(0, samples, start_fields, 0)

    for index in range(3):
        wsplit[index] = mixer_fine[:, index * channels : (index + 1) * channels]
    row = lax.broadcasted_iota(jnp.int32, (tokens, tokens), 0)
    col = lax.broadcasted_iota(jnp.int32, (tokens, tokens), 1)
    parity, rest = row // patch, row % patch
    quadrant, within = rest // piece, rest % piece
    origin = (
        quadrant * (half * half)
        + (2 * (within // quarter) + parity % 2) * half
        + 2 * (within % quarter)
        + parity // 2
    )
    perm_fine[...] = (origin == col).astype(F32).astype(BF16)
    row = lax.broadcasted_iota(jnp.int32, (patch, patch), 0)
    col = lax.broadcasted_iota(jnp.int32, (patch, patch), 1)
    down, across = row // half, row % half
    origin = (
        (down // quarter * 2 + across // quarter) * piece
        + (down % quarter) * quarter
        + across % quarter
    )
    perm_coarse[...] = (origin == col).astype(F32).astype(BF16)

    def home_copy(n, a, b):
        source = mbuf.at[n, a * 2 + b]
        target = mhome.at[n, (1 - a) * 2 + (1 - b)]
        if a == 0 and b == 0:
            return pltpu.make_async_copy(source, target, m_recv)
        return pltpu.make_async_remote_copy(
            source, target, m_send.at[n, a * 2 + b], m_recv,
            device_id=at(a, b), device_id_type=MESH,
        )

    def owner_copy(n, a, b):
        hx, hy = at(a, b)
        member = n % 4
        ox = hx - hx % 2 + member // 2
        oy = hy - hy % 2 + member % 2
        source = mbuf.at[n, a * 2 + b]
        target = cbuf.at[n // 4, (hx % 2) * 2 + hy % 2, (1 - a) * 2 + (1 - b)]
        here = jnp.logical_and(ox == x, oy == y)
        local = pltpu.make_async_copy(source, target, c_recv.at[n // 4])
        remote = pltpu.make_async_remote_copy(
            source, target, c_send.at[n, a * 2 + b], c_recv.at[n // 4],
            device_id=(ox, oy), device_id_type=MESH,
        )
        return here, local, remote

    def fine(n, carry):
        pltpu.make_async_copy(fbuf.at[n], fbuf.at[n], f_recv.at[n]).wait()
        window = fbuf[n].astype(F32).reshape(tokens, channels).astype(BF16)
        value = dot(perm_fine[...], window)
        normed = normalize(value, gain_window[...])
        q, k, v = (dot(normed, wsplit[index]).astype(BF16) for index in range(3))
        attended = (value + project(attention(q, k, v), output_fine)).astype(BF16).astype(F32)
        normed = normalize(attended, gain_hidden[...])
        hidden = gelu(dot(normed, expand[...])).astype(BF16)
        refined = (attended + dot(hidden, contract[...])).astype(BF16).astype(F32)
        slabs = [refined[p * patch : (p + 1) * patch] for p in range(4)]
        mean = sum(jnp.sum(s, -1, keepdims=True) for s in slabs) * (1.0 / (4 * channels))
        slabs = [s - mean for s in slabs]
        spread = sum(jnp.sum(s * s, -1, keepdims=True) for s in slabs) * (1.0 / (4 * channels))
        scale = lax.rsqrt(spread + EPSILON)
        merged = None
        for p, s in enumerate(slabs):
            gain = gain_merge[:, p * channels : (p + 1) * channels]
            part = dot(
                (s * scale * gain).astype(BF16), merge_weight[p * channels : (p + 1) * channels, :]
            )
            merged = part if merged is None else merged + part
        mbuf[n] = merged.astype(BF16).reshape(4, piece, wide)
        for a, b in ORDER:
            here, local, remote = owner_copy(n, a, b)
            pl.when(here)(local.start)
            pl.when(jnp.logical_not(here))(remote.start)
        for a, b in ORDER:
            home_copy(n, a, b).start()
        return carry

    lax.fori_loop(0, samples, fine, 0)

    bx, by = x - x % 2, y - y % 2
    me = (x % 2) * 2 + y % 2

    def result_copy(s, home):
        hx, hy = bx + home // 2, by + home % 2
        n = s * 4 + me
        local = pltpu.make_async_copy(obuf.at[s, home], coarse_out.at[n], o_recv)
        remote = pltpu.make_async_remote_copy(
            obuf.at[s, home], coarse_out.at[n], o_send.at[s, home], o_recv,
            device_id=(hx, hy), device_id_type=MESH,
        )
        return home == me, local, remote

    def coarse(s, carry):
        pltpu.make_async_copy(cbuf.at[s], cbuf.at[s], c_recv.at[s]).wait()
        merged = cbuf[s].reshape(4 * patch, wide).astype(F32)
        normed = normalize(merged, gain_coarse[...])
        q, k, v = (
            dot(normed, mixer_coarse[:, index * wide : (index + 1) * wide]).astype(BF16)
            for index in range(3)
        )
        out = (merged + project(attention(q, k, v), output_coarse)).astype(BF16)
        for home in range(4):
            obuf[s, home] = dot(
                perm_coarse[...], out[home * patch : (home + 1) * patch]
            ).astype(BF16)
            here, local, remote = result_copy(s, home)
            pl.when(here)(local.start)
            pl.when(jnp.logical_not(here))(remote.start)
        return carry

    lax.fori_loop(0, samples // 4, coarse, 0)

    pltpu.make_async_copy(mhome, mhome, m_recv).wait()

    def settle(n, carry):
        merged_out[n] = dot(perm_coarse[...], mhome[n].reshape(patch, wide)).astype(BF16)
        for a, b in ORDER:
            if (a, b) != (1, 1):
                field_copy(n, a, b).wait_send()
            if (a, b) != (0, 0):
                home_copy(n, a, b).wait_send()
            here, _, remote = owner_copy(n, a, b)
            pl.when(jnp.logical_not(here))(remote.wait_send)
        return carry

    lax.fori_loop(0, samples, settle, 0)
    for s in range(samples // 4):
        for home in range(4):
            here, _, remote = result_copy(s, home)
            pl.when(jnp.logical_not(here))(remote.wait_send)
    pltpu.make_async_copy(coarse_out, coarse_out, o_recv).wait()


def shards(nx, ny, fields, *weights):
    samples, side, _, channels = fields.shape
    half = side // 2
    wide = weights[7].shape[-1]
    piece = half * half // 4
    weights = [w.reshape(1, -1) if w.ndim == 1 else w for w in weights]
    shape = jax.ShapeDtypeStruct((samples, 4 * piece, wide), BF16)
    vmem = pl.BlockSpec(memory_space=pltpu.VMEM)
    hbm = pl.BlockSpec(memory_space=pl.ANY)
    dma = pltpu.SemaphoreType.DMA
    merged, coarse = pl.pallas_call(
        functools.partial(kernel, nx, ny),
        out_shape=(shape, shape),
        in_specs=[hbm] + [vmem] * len(weights),
        out_specs=(vmem, hbm),
        scratch_shapes=[
            pltpu.VMEM((samples, 4, half, half, channels), BF16),
            pltpu.VMEM((samples, 4, piece, wide), BF16),
            pltpu.VMEM((samples, 4, piece, wide), BF16),
            pltpu.VMEM((samples // 4, 4, 4, piece, wide), BF16),
            pltpu.VMEM((samples // 4, 4, 4 * piece, wide), BF16),
            pltpu.VMEM((3, channels, channels), BF16),
            pltpu.VMEM((side * side, side * side), BF16),
            pltpu.VMEM((4 * piece, 4 * piece), BF16),
            dma((samples, 4)), dma((samples,)),
            dma((samples, 4)), dma,
            dma((samples, 4)), dma((samples // 4,)),
            dma((samples // 4, 4)), dma,
        ],
        compiler_params=pltpu.CompilerParams(
            collective_id=0, has_side_effects=True, vmem_limit_bytes=48 * 1024 * 1024
        ),
        name="encoder",
    )(fields.reshape(samples, side, 2, half, channels), *weights)
    return tuple(t.reshape(samples, half, half, wide) for t in (merged, coarse))


def solution(mesh):
    in_specs = (P(None, "gx", "gy", None),) + (P(),) * 11
    out_specs = (P(None, "gx", "gy", None), P(None, "gx", "gy", None))
    body = functools.partial(shards, mesh.shape["gx"], mesh.shape["gy"])
    return jax.shard_map(body, mesh=mesh, in_specs=in_specs, out_specs=out_specs, check_vma=False)
```

time: 136 us -> 52.7 us (0.39); the launches traced: 134 us -> 52.3 us
  matrix products: 50.1 us -> 0 us
  waiting for transfers between devices: 44.3 us -> 0 us
  Pallas kernels: 0 us -> 42.3 us
  local copies, waits for them, and re-layouts: 20.4 us -> 9.36 us
  starting transfers between devices: 9.69 us -> 0 us
  other arithmetic: 8.07 us -> 0 us
    ppermute x6 -> x0, waiting for transfers between devices: 44.3 us -> none  [the longest x4 36.7 us: from_behind(): lax.ppermute(shard, axis, [(i, (i + by) % count) for i in range(count)])]
    pallas_call x0 -> x1, Pallas kernels: none -> 42.3 us  [shards(): pl.pallas_call(functools.partial(kernel, nx, ny), out_shape=(shape, shape...]
    dot_general x10 -> x0, matrix products: 36.8 us -> none  [the longest x1 16 us: feed_forward(): jnp.dot(hidden, contract, preferred_element_type=jnp.float32)]
    sub x2 -> x0, matrix products: 13.3 us -> none  [attend(): powers = jnp.exp(scores - highest)]
    convert_element_type x6 -> x0, local copies, waits for them, and re-layouts: 11.7 us -> none  [the longest x3 9.16 us: normalize(): values = values.astype(jnp.float32)]
    ppermute x6 -> x0, starting transfers between devices: 9.69 us -> none  [the longest x4 8.75 us: from_behind(): lax.ppermute(shard, axis, [(i, (i + by) % count) for i in range(count)])]
    slice x6 -> x0, local copies, waits for them, and re-layouts: 7.57 us -> none  [the longest x2 4.22 us: shards(): gathered[..., :coarse_width]]
    unnamed x30 -> x21, local copies, waits for them, and re-layouts: 0.74 us -> 7.93 us
  transfers between devices with their start and end apart: 6 -> 0, of which waited for: 6 -> 0; matrix products, arithmetic and copies ran while one was open for 1% -> 0% of each run, Pallas kernels for 0% -> 0%
where the time goes in v1:
time: 52.7 us; the launch traced here: 52.3 us
  Pallas kernels  42.3 us (80%)
  local copies, waits for them, and re-layouts  9.36 us (18%)
  between operations  0.7 us (1%)
    pallas_call x1, Pallas kernels, shards(): pl.pallas_call(functools.partial(kernel, nx, ny), out_shape=(shape, shape...  42.3 us
    unnamed x21, local copies, waits for them, and re-layouts  7.93 us
    reshape x2, local copies, waits for them, and re-layouts, shards(): weights = [w.reshape(1, -1) if w.ndim == 1 else w for w in weights]  1.43 us

profile of v1, /device:TPU:0, one launch (start us, length us, event | category | flops | bytes accessed | tf_op | source)
XLA Modules:
  0.0 52.3 jit_solution(15280392692201555347)
XLA Ops:
  0.6 0.0 copy-start.2
  0.6 0.7 %reshape.29.gain_coarse = f32[1,384]{1,0:T(1,128)S(1)} reshape(f32[384]{0:T(512)} %param.21) | data formatting | bytes 3072 | tf_op jit(solution)/shard_map/reshape | solution.py:252
  1.4 0.7 %reshape.28.gain_merge = f32[1,768]{1,0:T(1,128)S(1)} reshape(f32[768]{0:T(1024)} %param.19) | data formatting | bytes 6144 | tf_op jit(solution)/shard_map/reshape | solution.py:252
  2.1 0.0 copy-start.6
  2.1 0.0 copy-start.7
  2.1 0.0 copy-start.8
  2.1 1.2 %copy.14.contract = bf16[768,192]{1,0:T(8,128)(2,1)S(1)} copy(bf16[768,192]{0,1:T(8,128)(2,1)} %param.18) | data formatting | bytes 589824 | tf_op args[6]
  3.3 0.0 copy-done.2
  3.3 0.0 copy-done.6
  3.3 0.0 copy-done.7
  3.3 0.0 copy-done.8
  3.3 0.0 copy-start
  3.3 1.2 %copy-done = bf16[8,16,16,192]{3,2,1,0:T(8,128)(2,1)S(1)} copy-done((bf16[8,16,16,192]{3,2,1,0:T(8,128)(2,1)S(1)}, bf16[8,16,16,192]{3,2,1,0:T(8,128)(2,1)}, u32[]{:S(2)}) %copy-start) | copy-done | bytes 786456
  4.5 0.0 copy-start.1
  4.5 1.2 %copy-done.1 = bf16[384,1152]{1,0:T(8,128)(2,1)S(1)} copy-done((bf16[384,1152]{1,0:T(8,128)(2,1)S(1)}, bf16[384,1152]{1,0:T(8,128)(2,1)}, u32[]{:S(2)}) %copy-start.1) | copy-done | bytes 884760
  5.7 0.0 copy-start.3
  5.7 1.0 %copy-done.3 = bf16[192,768]{1,0:T(8,128)(2,1)S(1)} copy-done((bf16[192,768]{1,0:T(8,128)(2,1)S(1)}, bf16[192,768]{1,0:T(8,128)(2,1)}, u32[]{:S(2)}) %copy-start.3) | copy-done | bytes 294936
  6.7 0.0 copy-start.4
  6.7 1.0 %copy-done.4 = bf16[384,384]{1,0:T(8,128)(2,1)S(1)} copy-done((bf16[384,384]{1,0:T(8,128)(2,1)S(1)}, bf16[384,384]{1,0:T(8,128)(2,1)}, u32[]{:S(2)}) %copy-start.4) | copy-done | bytes 294936
  7.6 0.0 copy-start.5
  7.6 0.9 %copy-done.5 = bf16[192,576]{1,0:T(8,128)(2,1)S(1)} copy-done((bf16[192,576]{1,0:T(8,128)(2,1)S(1)}, bf16[192,576]{1,0:T(8,128)(2,1)}, u32[]{:S(2)}) %copy-start.5) | copy-done | bytes 221208
  8.6 42.3 %encoder.1 = (bf16[8,64,384]{2,1,0:T(8,128)(2,1)S(1)}, bf16[8,64,384]{2,1,0:T(8,128)(2,1)S(1)}) custom-call(bf16[8,16,2,8,192]{4,3,2,1,0:T(8,128)(2,1)S(1)} %bitcast.5, f32[1,192]{1,0:T(1,128)S(1)} %bitcast.8, bf16[192,576]{1,0:T(8,128)(2,1)S(1)} %copy-done.5, bf16[192,192]{1,0:T(8,128)(2,1)S(1)} %copy-done.6, f32[1,192]{1,0:T(1,128)S(1)} %bitcast.9, ...), custom_call_target="tpu_custom_call" | custom-call | tf_op jit(solution)/shard_map/encoder/pallas_call | solution.py:257
  50.8 0.7 %copy.17 = bf16[8,8,8,384]{3,2,1,0:T(8,128)(2,1)} copy(bf16[8,8,8,384]{3,2,1,0:T(8,128)(2,1)S(1)} %bitcast.7) | data formatting | bytes 786432
  51.6 0.7 %copy.18 = bf16[8,8,8,384]{3,2,1,0:T(8,128)(2,1)} copy(bf16[8,8,8,384]{3,2,1,0:T(8,128)(2,1)S(1)} %bitcast.6) | data formatting | bytes 786432
Async XLA Ops:
  0.6 2.6 %copy-start.2 = (bf16[768,384]{1,0:T(8,128)(2,1)S(1)}, bf16[768,384]{1,0:T(8,128)(2,1)}, u32[]{:S(2)}) copy-start(bf16[768,384]{1,0:T(8,128)(2,1)} %merge_weight.1) | copy-start | bytes 1769476
  2.1 1.2 %copy-start.6 = (bf16[192,192]{1,0:T(8,128)(2,1)S(1)}, bf16[192,192]{1,0:T(8,128)(2,1)}, u32[]{:S(2)}) copy-start(bf16[192,192]{1,0:T(8,128)(2,1)} %output_fine.1) | copy-start | bytes 221188
  2.1 1.2 %copy-start.7 = (f32[192]{0:T(256)S(1)}, f32[192]{0:T(256)}, u32[]{:S(2)}) copy-start(f32[192]{0:T(256)} %param.13) | copy-start | bytes 2308
  2.1 1.2 %copy-start.8 = (f32[192]{0:T(256)S(1)}, f32[192]{0:T(256)}, u32[]{:S(2)}) copy-start(f32[192]{0:T(256)} %param.16) | copy-start | bytes 2308
  3.3 1.2 %copy-start = (bf16[8,16,16,192]{3,2,1,0:T(8,128)(2,1)S(1)}, bf16[8,16,16,192]{3,2,1,0:T(8,128)(2,1)}, u32[]{:S(2)}) copy-start(bf16[8,16,16,192]{3,2,1,0:T(8,128)(2,1)} %param.12) | copy-start | bytes 2359300
  4.5 1.2 %copy-start.1 = (bf16[384,1152]{1,0:T(8,128)(2,1)S(1)}, bf16[384,1152]{1,0:T(8,128)(2,1)}, u32[]{:S(2)}) copy-start(bf16[384,1152]{1,0:T(8,128)(2,1)} %mixer_coarse.1) | copy-start | bytes 2654212
  5.7 1.0 %copy-start.3 = (bf16[192,768]{1,0:T(8,128)(2,1)S(1)}, bf16[192,768]{1,0:T(8,128)(2,1)}, u32[]{:S(2)}) copy-start(bf16[192,768]{1,0:T(8,128)(2,1)} %expand.1) | copy-start | bytes 884740
  6.7 1.0 %copy-start.4 = (bf16[384,384]{1,0:T(8,128)(2,1)S(1)}, bf16[384,384]{1,0:T(8,128)(2,1)}, u32[]{:S(2)}) copy-start(bf16[384,384]{1,0:T(8,128)(2,1)} %output_coarse.1) | copy-start | bytes 884740
  7.6 0.9 %copy-start.5 = (bf16[192,576]{1,0:T(8,128)(2,1)S(1)}, bf16[192,576]{1,0:T(8,128)(2,1)}, u32[]{:S(2)}) copy-start(bf16[192,576]{1,0:T(8,128)(2,1)} %mixer_fine.1) | copy-start | bytes 663556

commit v2 on v1

--- a/solution.py
+++ b/solution.py
@@ -18,6 +18,10 @@
 
 def dot(a, b):
     return jnp.dot(a, b, preferred_element_type=F32)
+
+
+def dot_nt(a, b):
+    return lax.dot_general(a, b, (((1,), (1,)), ((), ())), preferred_element_type=F32)
 
 
 def normalize(values, gain):
@@ -41,10 +45,7 @@
         context = None
         for head in range(width // HEAD):
             mine = owner == head
-            scores = lax.dot_general(
-                q * mine.astype(F32).astype(BF16), k, (((1,), (1,)), ((), ())),
-                preferred_element_type=F32,
-            )
+            scores = dot_nt(q * mine.astype(F32).astype(BF16), k)
             highest = jnp.max(scores, -1, keepdims=True)
             powers = jnp.exp2((scores - highest) * factor)
             total = jnp.sum(powers, -1, keepdims=True)
@@ -64,25 +65,43 @@
 
 def kernel(
     nx, ny,
-    fields, gain_window, mixer_fine, output_fine, gain_hidden, expand, contract,
-    gain_merge, merge_weight, gain_coarse, mixer_coarse, output_coarse,
-    merged_out, coarse_out,
-    fbuf, mbuf, mhome, cbuf, obuf, wsplit, perm_fine, perm_coarse,
+    fields, *refs
+):
+    count = (len(refs) - 16) // 2
+    weights_hbm, (mhome, coarse_out) = refs[:count], refs[count : count + 2]
+    weights = refs[count + 2 : 2 * count + 2]
+    (
+        gain_window, mixer_fine, output_fine, gain_hidden, expand, contract,
+        gain_merge, merge_weight, gain_coarse, mixer_coarse, output_coarse,
+    ) = weights
+    (
+    fbuf, mbuf, cbuf, obuf, wsplit, perm_fine,
     f_send, f_recv, m_send, m_recv, c_send, c_recv, o_send, o_recv,
-):
+    w_recv,
+    ) = refs[2 * count + 2 :]
     samples, _, half, _, channels = fbuf.shape
     side = 2 * half
     tokens = side * side
     quarter = half // 2
     piece = quarter * quarter
     patch = 4 * piece
-    wide = merged_out.shape[-1]
+    wide = mhome.shape[-1]
     x = lax.axis_index("gx")
     y = lax.axis_index("gy")
 
     def at(dx, dy):
         return (lax.rem(x + dx + nx, nx), lax.rem(y + dy + ny, ny))
 
+    reach = [(dx, dy) for dx in (-1, 0, 1) for dy in (-1, 0, 1) if (dx, dy) != (0, 0)]
+    barrier = pltpu.get_barrier_semaphore()
+    for dx, dy in reach:
+        pl.semaphore_signal(barrier, inc=1, device_id=at(dx, dy), device_id_type=MESH)
+    loads = [
+        pltpu.make_async_copy(source, target, w_recv.at[index])
+        for index, (source, target) in enumerate(zip(weights_hbm, weights))
+    ]
+    for load in loads:
+        load.start()
     def field_copy(n, a, b):
         slot = (1 - a) * 2 + (1 - b)
         source = fields.at[n, pl.ds(a * half, half), b]
@@ -96,10 +115,6 @@
 
     ORDER = ((0, 0), (0, 1), (1, 0), (1, 1))
 
-    barrier = pltpu.get_barrier_semaphore()
-    reach = [(dx, dy) for dx in range(-2, 3) for dy in range(-2, 3) if (dx, dy) != (0, 0)]
-    for dx, dy in reach:
-        pl.semaphore_signal(barrier, inc=1, device_id=at(dx, dy), device_id_type=MESH)
     pl.semaphore_wait(barrier, len(reach))
 
     def start_fields(n, carry):
@@ -107,8 +122,11 @@
             field_copy(n, a, b).start()
         return carry
 
-    lax.fori_loop(0, samples, start_fields, 0)
-
+    ahead = min(3, samples)
+    lax.fori_loop(0, ahead, start_fields, 0)
+
+    for load in loads[:8]:
+        load.wait()
     for index in range(3):
         wsplit[index] = mixer_fine[:, index * channels : (index + 1) * channels]
     row = lax.broadcasted_iota(jnp.int32, (tokens, tokens), 0)
@@ -122,16 +140,6 @@
         + parity // 2
     )
     perm_fine[...] = (origin == col).astype(F32).astype(BF16)
-    row = lax.broadcasted_iota(jnp.int32, (patch, patch), 0)
-    col = lax.broadcasted_iota(jnp.int32, (patch, patch), 1)
-    down, across = row // half, row % half
-    origin = (
-        (down // quarter * 2 + across // quarter) * piece
-        + (down % quarter) * quarter
-        + across % quarter
-    )
-    perm_coarse[...] = (origin == col).astype(F32).astype(BF16)
-
     def home_copy(n, a, b):
         source = mbuf.at[n, a * 2 + b]
         target = mhome.at[n, (1 - a) * 2 + (1 - b)]
@@ -158,15 +166,19 @@
         return here, local, remote
 
     def fine(n, carry):
+        @pl.when(n + ahead < samples)
+        def _():
+            start_fields(n + ahead, 0)
+
         pltpu.make_async_copy(fbuf.at[n], fbuf.at[n], f_recv.at[n]).wait()
         window = fbuf[n].astype(F32).reshape(tokens, channels).astype(BF16)
         value = dot(perm_fine[...], window)
-        normed = normalize(value, gain_window[...])
+        normed = normalize(value, gain_window[...][None])
         q, k, v = (dot(normed, wsplit[index]).astype(BF16) for index in range(3))
         attended = (value + project(attention(q, k, v), output_fine)).astype(BF16).astype(F32)
-        normed = normalize(attended, gain_hidden[...])
+        normed = normalize(attended, gain_hidden[...][None])
         hidden = gelu(dot(normed, expand[...])).astype(BF16)
-        refined = (attended + dot(hidden, contract[...])).astype(BF16).astype(F32)
+        refined = (attended + dot_nt(hidden, contract[...])).astype(BF16).astype(F32)
         slabs = [refined[p * patch : (p + 1) * patch] for p in range(4)]
         mean = sum(jnp.sum(s, -1, keepdims=True) for s in slabs) * (1.0 / (4 * channels))
         slabs = [s - mean for s in slabs]
@@ -174,7 +186,7 @@
         scale = lax.rsqrt(spread + EPSILON)
         merged = None
         for p, s in enumerate(slabs):
-            gain = gain_merge[:, p * channels : (p + 1) * channels]
+            gain = gain_merge[...][None, p * channels : (p + 1) * channels]
             part = dot(
                 (s * scale * gain).astype(BF16), merge_weight[p * channels : (p + 1) * channels, :]
             )
@@ -206,27 +218,26 @@
     def coarse(s, carry):
         pltpu.make_async_copy(cbuf.at[s], cbuf.at[s], c_recv.at[s]).wait()
         merged = cbuf[s].reshape(4 * patch, wide).astype(F32)
-        normed = normalize(merged, gain_coarse[...])
+        normed = normalize(merged, gain_coarse[...][None])
         q, k, v = (
             dot(normed, mixer_coarse[:, index * wide : (index + 1) * wide]).astype(BF16)
             for index in range(3)
         )
         out = (merged + project(attention(q, k, v), output_coarse)).astype(BF16)
         for home in range(4):
-            obuf[s, home] = dot(
-                perm_coarse[...], out[home * patch : (home + 1) * patch]
-            ).astype(BF16)
+            obuf[s, home] = out[home * patch : (home + 1) * patch]
             here, local, remote = result_copy(s, home)
             pl.when(here)(local.start)
             pl.when(jnp.logical_not(here))(remote.start)
         return carry
 
+    for load in loads[8:]:
+        load.wait()
     lax.fori_loop(0, samples // 4, coarse, 0)
 
     pltpu.make_async_copy(mhome, mhome, m_recv).wait()
 
     def settle(n, carry):
-        merged_out[n] = dot(perm_coarse[...], mhome[n].reshape(patch, wide)).astype(BF16)
         for a, b in ORDER:
             if (a, b) != (1, 1):
                 field_copy(n, a, b).wait_send()
@@ -244,40 +255,67 @@
     pltpu.make_async_copy(coarse_out, coarse_out, o_recv).wait()
 
 
+def natural_order(half, merged, coarse, merged_out, coarse_out):
+    quarter = half // 2
+    piece = quarter * quarter
+    patch = 4 * piece
+    row = lax.broadcasted_iota(jnp.int32, (patch, patch), 0)
+    col = lax.broadcasted_iota(jnp.int32, (patch, patch), 1)
+    down, across = row // half, row % half
+    origin = (
+        (down // quarter * 2 + across // quarter) * piece
+        + (down % quarter) * quarter
+        + across % quarter
+    )
+    order = (origin == col).astype(F32).astype(BF16)
+    for n in range(merged.shape[0]):
+        merged_out[n] = dot(order, merged[n]).astype(BF16)
+        coarse_out[n] = dot(order, coarse[n]).astype(BF16)
+
+
 def shards(nx, ny, fields, *weights):
     samples, side, _, channels = fields.shape
     half = side // 2
     wide = weights[7].shape[-1]
     piece = half * half // 4
-    weights = [w.reshape(1, -1) if w.ndim == 1 else w for w in weights]
+    weights = [*weights[:5], weights[5].T, *weights[6:]]
+    pieces = jax.ShapeDtypeStruct((samples, 4, piece, wide), BF16)
     shape = jax.ShapeDtypeStruct((samples, 4 * piece, wide), BF16)
-    vmem = pl.BlockSpec(memory_space=pltpu.VMEM)
     hbm = pl.BlockSpec(memory_space=pl.ANY)
     dma = pltpu.SemaphoreType.DMA
     merged, coarse = pl.pallas_call(
         functools.partial(kernel, nx, ny),
-        out_shape=(shape, shape),
-        in_specs=[hbm] + [vmem] * len(weights),
-        out_specs=(vmem, hbm),
-        scratch_shapes=[
+        out_shape=(pieces, shape),
+        in_specs=[hbm] * (1 + len(weights)),
+        out_specs=(hbm, hbm),
+        scratch_shapes=[pltpu.VMEM(w.shape, w.dtype) for w in weights] + [
             pltpu.VMEM((samples, 4, half, half, channels), BF16),
-            pltpu.VMEM((samples, 4, piece, wide), BF16),
             pltpu.VMEM((samples, 4, piece, wide), BF16),
             pltpu.VMEM((samples // 4, 4, 4, piece, wide), BF16),
             pltpu.VMEM((samples // 4, 4, 4 * piece, wide), BF16),
             pltpu.VMEM((3, channels, channels), BF16),
             pltpu.VMEM((side * side, side * side), BF16),
-            pltpu.VMEM((4 * piece, 4 * piece), BF16),
             dma((samples, 4)), dma((samples,)),
             dma((samples, 4)), dma,
             dma((samples, 4)), dma((samples // 4,)),
             dma((samples // 4, 4)), dma,
+            dma((len(weights),)),
         ],
         compiler_params=pltpu.CompilerParams(
-            collective_id=0, has_side_effects=True, vmem_limit_bytes=48 * 1024 * 1024
+            collective_id=0, has_side_effects=True, vmem_limit_bytes=62 * 1024 * 1024
         ),
         name="encoder",
     )(fields.reshape(samples, side, 2, half, channels), *weights)
+    steps = 2
+    block = pl.BlockSpec((samples // steps, 4 * piece, wide), lambda step: (step, 0, 0))
+    merged, coarse = pl.pallas_call(
+        functools.partial(natural_order, half),
+        grid=(steps,),
+        out_shape=(shape, shape),
+        in_specs=[block] * 2,
+        out_specs=(block, block),
+        name="natural_order",
+    )(merged.reshape(shape.shape), coarse)
     return tuple(t.reshape(samples, half, half, wide) for t in (merged, coarse))
 
 

time: 52.7 us -> 45.4 us (0.86)
  local copies, waits for them, and re-layouts: 9.36 us -> 0 us
  Pallas kernels: 42.3 us -> 44.6 us
    unnamed x21 -> x0, local copies, waits for them, and re-layouts: 7.93 us -> none
    pallas_call x1 -> x2, Pallas kernels: 42.3 us -> 44.6 us  [the longest x1 42.3 us: shards(): pl.pallas_call(functools.partial(kernel, nx, ny), out_shape=(pieces, shap...]
    reshape x2 -> x0, local copies, waits for them, and re-layouts: 1.43 us -> none  [shards(): weights = [w.reshape(1, -1) if w.ndim == 1 else w for w in weights]]
where the time goes in v2:
time: 45.4 us; the launch traced here: 45.3 us
  Pallas kernels  44.6 us (98%)
  between operations  0.64 us (1%)
    pallas_call x1, Pallas kernels, shards(): pl.pallas_call(functools.partial(kernel, nx, ny), out_shape=(pieces, shap...  42.3 us
    pallas_call x1, Pallas kernels, shards(): pl.pallas_call(functools.partial(natural_order, half), grid=(steps,), out...  2.29 us

profile of v2, /device:TPU:0, one launch (start us, length us, event | category | flops | bytes accessed | tf_op | source)
XLA Modules:
  0.0 45.3 jit_solution(15100046836528527427)
XLA Ops:
  0.6 42.3 %encoder.1 = (bf16[8,4,16,384]{3,2,1,0:T(8,128)(2,1)}, bf16[8,64,384]{2,1,0:T(8,128)(2,1)}) custom-call(bf16[8,16,2,8,192]{4,3,2,1,0:T(8,128)(2,1)} %bitcast.5, f32[192]{0:T(256)} %refs_0_.1, bf16[192,576]{1,0:T(8,128)(2,1)} %refs_1_.1, bf16[192,192]{1,0:T(8,128)(2,1)} %refs_2_.1, f32[192]{0:T(256)} %refs_3_.1, bf16[192,768]{1,0:T(8,128)(2,1)} %refs_4_.1, ...), custom_call_target="tpu_custom_call" | custom-call | tf_op jit(solution)/shard_map/encoder/pallas_call | solution.py:286
  43.0 2.3 %natural_order.1 = (bf16[8,64,384]{2,1,0:T(8,128)(2,1)}, bf16[8,64,384]{2,1,0:T(8,128)(2,1)}) custom-call(bf16[8,64,384]{2,1,0:T(8,128)(2,1)} %bitcast.6, bf16[8,64,384]{2,1,0:T(8,128)(2,1)} %get-tuple-element.7.coarse), custom_call_target="tpu_custom_call" | custom-call | tf_op jit(solution)/shard_map/natural_order/pallas_call | solution.py:311

commit v3 on v2

--- a/solution.py
+++ b/solution.py
@@ -122,7 +122,7 @@
             field_copy(n, a, b).start()
         return carry
 
-    ahead = min(3, samples)
+    ahead = min(4, samples)
     lax.fori_loop(0, ahead, start_fields, 0)
 
     for load in loads[:8]:
@@ -165,21 +165,41 @@
         )
         return here, local, remote
 
-    def fine(n, carry):
-        @pl.when(n + ahead < samples)
-        def _():
-            start_fields(n + ahead, 0)
-
-        pltpu.make_async_copy(fbuf.at[n], fbuf.at[n], f_recv.at[n]).wait()
-        window = fbuf[n].astype(F32).reshape(tokens, channels).astype(BF16)
-        value = dot(perm_fine[...], window)
+    group = 2
+
+    def fine(step, carry):
+        first = step * group
+
+        for w in range(group):
+            @pl.when(first + w + ahead < samples)
+            def _():
+                start_fields(first + w + ahead, 0)
+
+        values = []
+        for w in range(group):
+            n = first + w
+            pltpu.make_async_copy(fbuf.at[n], fbuf.at[n], f_recv.at[n]).wait()
+            window = fbuf[n].astype(F32).reshape(tokens, channels).astype(BF16)
+            values.append(dot(perm_fine[...], window))
+        value = jnp.concatenate(values, axis=0)
         normed = normalize(value, gain_window[...][None])
         q, k, v = (dot(normed, wsplit[index]).astype(BF16) for index in range(3))
-        attended = (value + project(attention(q, k, v), output_fine)).astype(BF16).astype(F32)
+        parts = [
+            attention(*(t[w * tokens : (w + 1) * tokens] for t in (q, k, v)))
+            for w in range(group)
+        ]
+        context = [jnp.concatenate(c, axis=0) for c in zip(*parts)]
+        attended = (value + project(context, output_fine)).astype(BF16).astype(F32)
         normed = normalize(attended, gain_hidden[...][None])
         hidden = gelu(dot(normed, expand[...])).astype(BF16)
         refined = (attended + dot_nt(hidden, contract[...])).astype(BF16).astype(F32)
-        slabs = [refined[p * patch : (p + 1) * patch] for p in range(4)]
+        slabs = [
+            jnp.concatenate(
+                [refined[w * tokens + p * patch : w * tokens + (p + 1) * patch] for w in range(group)],
+                axis=0,
+            )
+            for p in range(4)
+        ]
         mean = sum(jnp.sum(s, -1, keepdims=True) for s in slabs) * (1.0 / (4 * channels))
         slabs = [s - mean for s in slabs]
         spread = sum(jnp.sum(s * s, -1, keepdims=True) for s in slabs) * (1.0 / (4 * channels))
@@ -191,16 +211,19 @@
                 (s * scale * gain).astype(BF16), merge_weight[p * channels : (p + 1) * channels, :]
             )
             merged = part if merged is None else merged + part
-        mbuf[n] = merged.astype(BF16).reshape(4, piece, wide)
-        for a, b in ORDER:
-            here, local, remote = owner_copy(n, a, b)
-            pl.when(here)(local.start)
-            pl.when(jnp.logical_not(here))(remote.start)
-        for a, b in ORDER:
-            home_copy(n, a, b).start()
+        merged = merged.astype(BF16)
+        for w in range(group):
+            n = first + w
+            mbuf[n] = merged[w * patch : (w + 1) * patch].reshape(4, piece, wide)
+            for a, b in ORDER:
+                here, local, remote = owner_copy(n, a, b)
+                pl.when(here)(local.start)
+                pl.when(jnp.logical_not(here))(remote.start)
+            for a, b in ORDER:
+                home_copy(n, a, b).start()
         return carry
 
-    lax.fori_loop(0, samples, fine, 0)
+    lax.fori_loop(0, samples // group, fine, 0)
 
     bx, by = x - x % 2, y - y % 2
     me = (x % 2) * 2 + y % 2
@@ -215,20 +238,26 @@
         )
         return home == me, local, remote
 
+    sides = (1 - x % 2, x % 2)
+
     def coarse(s, carry):
         pltpu.make_async_copy(cbuf.at[s], cbuf.at[s], c_recv.at[s]).wait()
-        merged = cbuf[s].reshape(4 * patch, wide).astype(F32)
+        merged = jnp.concatenate(
+            [cbuf[s, pl.ds(2 * part, 2)].reshape(2 * patch, wide) for part in sides], axis=0
+        ).astype(F32)
         normed = normalize(merged, gain_coarse[...][None])
         q, k, v = (
             dot(normed, mixer_coarse[:, index * wide : (index + 1) * wide]).astype(BF16)
             for index in range(3)
         )
-        out = (merged + project(attention(q, k, v), output_coarse)).astype(BF16)
-        for home in range(4):
-            obuf[s, home] = out[home * patch : (home + 1) * patch]
-            here, local, remote = result_copy(s, home)
-            pl.when(here)(local.start)
-            pl.when(jnp.logical_not(here))(remote.start)
+        for index, part in enumerate(sides):
+            rows = slice(index * 2 * patch, (index + 1) * 2 * patch)
+            out = merged[rows] + project(attention(q[rows], k, v), output_coarse)
+            obuf[s, pl.ds(2 * part, 2)] = out.astype(BF16).reshape(2, patch, wide)
+            for column in range(2):
+                here, local, remote = result_copy(s, 2 * part + column)
+                pl.when(here)(local.start)
+                pl.when(jnp.logical_not(here))(remote.start)
         return carry
 
     for load in loads[8:]:

time: 45.4 us -> 41 us (0.903)
  Pallas kernels: 44.6 us -> 39.8 us
    pallas_call x1, Pallas kernels: 42.3 us -> 37.6 us  [shards(): pl.pallas_call(functools.partial(kernel, nx, ny), out_shape=(pieces, shap...]
where the time goes in v3:
time: 41 us; the launch traced here: 40.5 us
  Pallas kernels  39.8 us (97%)
  between operations  0.64 us (2%)
    pallas_call x1, Pallas kernels, shards(): pl.pallas_call(functools.partial(kernel, nx, ny), out_shape=(pieces, shap...  37.6 us
    pallas_call x1, Pallas kernels, shards(): pl.pallas_call(functools.partial(natural_order, half), grid=(steps,), out...  2.29 us

profile of v3, /device:TPU:0, one launch (start us, length us, event | category | flops | bytes accessed | tf_op | source)
XLA Modules:
  0.0 40.5 jit_solution(13938463884976755549)
XLA Ops:
  0.6 37.6 %encoder.1 = (bf16[8,4,16,384]{3,2,1,0:T(8,128)(2,1)}, bf16[8,64,384]{2,1,0:T(8,128)(2,1)}) custom-call(bf16[8,16,2,8,192]{4,3,2,1,0:T(8,128)(2,1)} %bitcast.5, f32[192]{0:T(256)} %refs_0_.1, bf16[192,576]{1,0:T(8,128)(2,1)} %refs_1_.1, bf16[192,192]{1,0:T(8,128)(2,1)} %refs_2_.1, f32[192]{0:T(256)} %refs_3_.1, bf16[192,768]{1,0:T(8,128)(2,1)} %refs_4_.1, ...), custom_call_target="tpu_custom_call" | custom-call | tf_op jit(solution)/shard_map/encoder/pallas_call | solution.py:315
  38.2 2.3 %natural_order.1 = (bf16[8,64,384]{2,1,0:T(8,128)(2,1)}, bf16[8,64,384]{2,1,0:T(8,128)(2,1)}) custom-call(bf16[8,64,384]{2,1,0:T(8,128)(2,1)} %bitcast.6, bf16[8,64,384]{2,1,0:T(8,128)(2,1)} %get-tuple-element.7.coarse), custom_call_target="tpu_custom_call" | custom-call | tf_op jit(solution)/shard_map/natural_order/pallas_call | solution.py:340

commit v4 on v3

--- a/solution.py
+++ b/solution.py
@@ -30,13 +30,15 @@
     return (center * lax.rsqrt(spread + EPSILON) * gain).astype(BF16)
 
 
+QUERY_SCALE = math.log2(math.e) / math.sqrt(HEAD)
+
+
 def gelu(x):
     return 0.5 * x * (1.0 + lax.erf(x * (1.0 / math.sqrt(2.0))))
 
 
 def attention(queries, keys, values):
     channels = queries.shape[-1]
-    factor = math.log2(math.e) / math.sqrt(HEAD)
     groups = []
     for low in range(0, channels, LANES):
         width = min(LANES, channels - low)
@@ -47,7 +49,7 @@
             mine = owner == head
             scores = dot_nt(q * mine.astype(F32).astype(BF16), k)
             highest = jnp.max(scores, -1, keepdims=True)
-            powers = jnp.exp2((scores - highest) * factor)
+            powers = jnp.exp2(scores - highest)
             total = jnp.sum(powers, -1, keepdims=True)
             part = dot(powers.astype(BF16), v) * (1.0 / total)
             context = part if context is None else jnp.where(mine, part, context)
@@ -183,7 +185,8 @@
             values.append(dot(perm_fine[...], window))
         value = jnp.concatenate(values, axis=0)
         normed = normalize(value, gain_window[...][None])
-        q, k, v = (dot(normed, wsplit[index]).astype(BF16) for index in range(3))
+        q = (dot(normed, wsplit[0]) * QUERY_SCALE).astype(BF16)
+        k, v = (dot(normed, wsplit[index]).astype(BF16) for index in (1, 2))
         parts = [
             attention(*(t[w * tokens : (w + 1) * tokens] for t in (q, k, v)))
             for w in range(group)
@@ -246,9 +249,10 @@
             [cbuf[s, pl.ds(2 * part, 2)].reshape(2 * patch, wide) for part in sides], axis=0
         ).astype(F32)
         normed = normalize(merged, gain_coarse[...][None])
-        q, k, v = (
+        q = (dot(normed, mixer_coarse[:, :wide]) * QUERY_SCALE).astype(BF16)
+        k, v = (
             dot(normed, mixer_coarse[:, index * wide : (index + 1) * wide]).astype(BF16)
-            for index in range(3)
+            for index in (1, 2)
         )
         for index, part in enumerate(sides):
             rows = slice(index * 2 * patch, (index + 1) * 2 * patch)

time: 41 us -> 41 us (level)
  no operation moved by 1% of the time
where the time goes in v4:
time: 41 us; the launch traced here: 40.5 us
  Pallas kernels  39.9 us (97%)
  between operations  0.64 us (2%)
    pallas_call x1, Pallas kernels, shards(): pl.pallas_call(functools.partial(kernel, nx, ny), out_shape=(pieces, shap...  37.6 us
    pallas_call x1, Pallas kernels, shards(): pl.pallas_call(functools.partial(natural_order, half), grid=(steps,), out...  2.29 us

profile of v4, /device:TPU:0, one launch (start us, length us, event | category | flops | bytes accessed | tf_op | source)
XLA Modules:
  0.0 40.5 jit_solution(5421604351027788595)
XLA Ops:
  0.6 37.6 %encoder.1 = (bf16[8,4,16,384]{3,2,1,0:T(8,128)(2,1)}, bf16[8,64,384]{2,1,0:T(8,128)(2,1)}) custom-call(bf16[8,16,2,8,192]{4,3,2,1,0:T(8,128)(2,1)} %bitcast.5, f32[192]{0:T(256)} %refs_0_.1, bf16[192,576]{1,0:T(8,128)(2,1)} %refs_1_.1, bf16[192,192]{1,0:T(8,128)(2,1)} %refs_2_.1, f32[192]{0:T(256)} %refs_3_.1, bf16[192,768]{1,0:T(8,128)(2,1)} %refs_4_.1, ...), custom_call_target="tpu_custom_call" | custom-call | tf_op jit(solution)/shard_map/encoder/pallas_call | solution.py:319
  38.2 2.3 %natural_order.1 = (bf16[8,64,384]{2,1,0:T(8,128)(2,1)}, bf16[8,64,384]{2,1,0:T(8,128)(2,1)}) custom-call(bf16[8,64,384]{2,1,0:T(8,128)(2,1)} %bitcast.6, bf16[8,64,384]{2,1,0:T(8,128)(2,1)} %get-tuple-element.7.coarse), custom_call_target="tpu_custom_call" | custom-call | tf_op jit(solution)/shard_map/natural_order/pallas_call | solution.py:344
